TPU v7x, 256 devices: a whole 4x4x8 slice. The times are simulated.
256 devices in a mesh: chain: 8 (over y, core), cols: 32 (over x, z).
Axes of the slice: x: 4, y: 4, z: 8, core: 2. Of those that a mesh axis runs over, the one named last changes fastest.
Arguments:
- factor: float32 [4608, 4608], P(('chain', 'cols')), may hold values from -2 to 2, as said below
- right_side: float32 [4608, 16384], P('chain', 'cols'), may hold values from -6 to 6
- occ_order: int32 [64], replicated, may hold values from 0 to 63, each once
- cabs_order: int32 [256], replicated, may hold values from 0 to 255, each once
Outputs:
- fitted: float32 [64, 256, 4608], P('cols', None, 'chain')
Inputs may be any that keep to these rules, and one draw needn't show every extreme that they name: factor is lower triangular: zero above the diagonal, its diagonal between 1 and 2.
All inputs are finite; a program needn't handle non-finite values.
Results may differ from a plain program's by a relative error of at most 0.00017.
Values sent between devices are 32-bit elements; how exact they have to be, the bound alone decides.
No kernel may reach another device: no remote copies, remote signals or barrier semaphores. Data moves between devices by JAX's collectives and lax.ppermute only.
A program may use at most 128 MiB of HBM per device.

v0:
```python
import jax
import jax.numpy as jnp
from jax import lax
from jax.sharding import PartitionSpec as P


def from_root(value, axis, root):
    return lax.dynamic_index_in_dim(lax.all_gather(value, axis), root, 0, keepdims=False)


def product(left, right):
    return jnp.dot(left, right, precision=lax.Precision.HIGHEST, preferred_element_type=jnp.float32)


def per_device(factor, right_side, occ_order, cabs_order):
    chain_size = lax.axis_size("chain")
    position = lax.axis_index("chain")
    factor_row = lax.all_gather(factor, "cols", axis=0, tiled=True)
    aux_rows = factor_row.shape[0]
    diag_block = lax.dynamic_slice_in_dim(factor_row, position * aux_rows, aux_rows, 1)
    identity = jnp.eye(aux_rows, dtype=jnp.float32)
    inverse = jax.scipy.linalg.solve_triangular(diag_block, identity, lower=True)

    def settle(residual):
        return product(inverse, residual)

    def blank(residual):
        return jnp.zeros_like(residual)

    residual = right_side
    solution = jnp.zeros_like(right_side)
    for section in range(chain_size):
        solved = lax.cond(position == section, settle, blank, residual)
        solution = solution + solved
        if section + 1 < chain_size:
            arrived = from_root(solved, "chain", section)
            coupling = factor_row[:, section * aux_rows : (section + 1) * aux_rows]

            def lower_block(current, arrived=arrived, coupling=coupling):
                return current - product(coupling, arrived)

            def keep_block(current):
                return current

            residual = lax.cond(position > section, lower_block, keep_block, residual)
    occ_total = occ_order.shape[0]
    cabs_local = right_side.shape[1] // occ_total
    cols_size = lax.axis_size("cols")
    occ_local = occ_total // cols_size
    grid = solution.reshape(aux_rows, cabs_local, occ_total)
    grid = jnp.take(grid, occ_order, axis=2)
    grid = grid.reshape(aux_rows, cabs_local, cols_size, occ_local)
    grid = jnp.transpose(grid, (2, 3, 1, 0))
    moved = jnp.take(
        lax.all_to_all(grid, "cols", split_axis=0, concat_axis=2, tiled=True), cabs_order, axis=2
    )
    return moved.reshape(occ_local, moved.shape[2], aux_rows)


def solution(mesh):
    in_specs = (P(("chain", "cols"), None), P("chain", "cols"), P(), P())
    out_specs = P("cols", None, "chain")
    return jax.shard_map(
        per_device, mesh=mesh, in_specs=in_specs, out_specs=out_specs, check_vma=False
    )
```

profile of v0, /device:TPU:33, one launch (start us, length us, event | category | flops | bytes accessed | tf_op | source)
XLA Modules:
  0.0 740.3 jit_solution(2091140109980776723)
XLA Ops:
  9.3 128.3 %all-gather.31.cloned.1.call-done = f32[32,18,4608]{2,1,0:T(8,128)} async-done(((f32[1,18,4608]{2,1,0:T(8,128)}), f32[32,18,4608]{2,1,0:T(8,128)}) %all-gather.31.cloned.1.call-update) | async-done | bytes 10616848 | tf_op jit(solution)/shard_map/all_gather | solution.py:18
  137.6 11.4 %reshape.89 = f32[576,4608]{1,0:T(8,128)} reshape(f32[32,18,4608]{2,1,0:T(8,128)} %all-gather.31.cloned.1.call-done) | data formatting | bytes 21233664
  150.7 10.5 %while.1 = (s32[]{:T(128)}, f32[576,576]{1,0:T(8,128)S(1)}, s32[4,2]{0,1:T(2,128)S(1)}, f32[4,128,128]{2,1,0:T(8,128)}, s32[]{:T(128)}) while((s32[]{:T(128)}, f32[576,576]{1,0:T(8,128)S(1)}, s32[4,2]{0,1:T(2,128)S(1)}, f32[4,128,128]{2,1,0:T(8,128)}, s32[]{:T(128)}) %tuple.169), condition=%wide.while_cond, body=%wide.while_body.sunk | while | flops 2 | bytes 132705 | solution.py:22
  151.4 2.0 bitcast_dynamic-update-slice_fusion.2
  154.0 2.0 bitcast_dynamic-update-slice_fusion.2
  156.7 2.0 bitcast_dynamic-update-slice_fusion.2
  162.6 49.8 %custom-call.4 = f32[5,128,128]{1,2,0:T(8,128)} custom-call(f32[5,128,128]{2,1,0:T(8,128)S(1)} %pad_maximum_fusion), custom_call_target="InvertDiagBlocksLowerTriangular" | custom-call | tf_op jit(solution)/shard_map/jit(_solve_triangular)/triangular_solve | solution.py:22
  220.5 2.0 fusion.57
  224.1 56.9 %all-gather.17.cloned.1.call-done = f32[4608,512]{1,0:T(8,128)} async-done(((f32[576,512]{1,0:T(8,128)}), f32[4608,512]{1,0:T(8,128)}) %all-gather.17.cloned.1.call-update) | async-done | bytes 9437200 | tf_op jit(solution)/shard_map/all_gather | solution.py:8
  281.0 5.0 conditional.16
  281.2 4.8 fusion.2
  286.0 4.1 conditional.17
  286.0 4.1 fusion.84
  290.2 55.5 %all-gather.19.cloned.1.call-done = f32[4608,512]{1,0:T(8,128)} async-done(((f32[576,512]{1,0:T(8,128)}), f32[4608,512]{1,0:T(8,128)}) %all-gather.19.cloned.1.call-update) | async-done | bytes 9437200 | tf_op jit(solution)/shard_map/all_gather | solution.py:8
  347.0 63.7 %all-gather.21.cloned.1.call-done = f32[4608,512]{1,0:T(8,128)} async-done(((f32[576,512]{1,0:T(8,128)}), f32[4608,512]{1,0:T(8,128)}) %all-gather.21.cloned.1.call-update) | async-done | bytes 9437200 | tf_op jit(solution)/shard_map/all_gather | solution.py:8
  412.4 63.4 %all-gather.23.cloned.1.call-done = f32[4608,512]{1,0:T(8,128)} async-done(((f32[576,512]{1,0:T(8,128)}), f32[4608,512]{1,0:T(8,128)}) %all-gather.23.cloned.1.call-update) | async-done | bytes 9437200 | tf_op jit(solution)/shard_map/all_gather | solution.py:8
  477.1 64.9 %all-gather.25.cloned.1.call-done = f32[4608,512]{1,0:T(8,128)} async-done(((f32[576,512]{1,0:T(8,128)}), f32[4608,512]{1,0:T(8,128)}) %all-gather.25.cloned.1.call-update) | async-done | bytes 9437200 | tf_op jit(solution)/shard_map/all_gather | solution.py:8
  543.4 64.6 %all-gather.27.cloned.1.call-done = f32[4608,512]{1,0:T(8,128)} async-done(((f32[576,512]{1,0:T(8,128)}), f32[4608,512]{1,0:T(8,128)}) %all-gather.27.cloned.1.call-update) | async-done | bytes 9437200 | tf_op jit(solution)/shard_map/all_gather | solution.py:8
  609.4 63.8 %all-gather.29.cloned.1.call-done = f32[4608,512]{1,0:T(8,128)} async-done(((f32[576,512]{1,0:T(8,128)}), f32[4608,512]{1,0:T(8,128)}) %all-gather.29.cloned.1.call-update) | async-done | bytes 9437200 | tf_op jit(solution)/shard_map/all_gather | solution.py:8
  674.6 4.9 add_add_fusion
  682.6 9.9 %all-to-all-start = ((f32[32,2,8,576]{3,2,1,0:T(8,128)}), f32[32,2,8,576]{3,2,1,0:T(8,128)S(1)}, u32[]{:S(2)}, u32[]{:S(2)}) async-start(f32[32,2,8,576]{3,2,1,0:T(8,128)} %select_bitcast_fusion.1), calls=%async_computation | async-start | bytes 2621440 | tf_op jit(solution)/shard_map/all_to_all | solution.py:55
  692.5 34.0 %all-to-all-done = f32[32,2,8,576]{3,2,1,0:T(8,128)S(1)} async-done(((f32[32,2,8,576]{3,2,1,0:T(8,128)}), f32[32,2,8,576]{3,2,1,0:T(8,128)S(1)}, u32[]{:S(2)}, u32[]{:S(2)}) %all-to-all-start) | async-done | bytes 1179680 | tf_op jit(solution)/shard_map/all_to_all | solution.py:55
  727.5 2.2 gather_fusion.1
  730.8 2.2 copy.71
  (88 shorter events, 41.9 us)
Async XLA Ops:
  6.5 131.1 %all-gather.31.cloned.1.call-start = ((), (), s32[]{:S(2)}) async-start(), calls=%async_computation.8 | async-start | bytes 14598144 | tf_op jit(solution)/shard_map/all_gather | solution.py:18
  7.8 273.2 %all-gather.17.cloned.1.call-start = ((), (), s32[]{:S(2)}) async-start(), calls=%async_computation.1 | async-start | bytes 10616832 | tf_op jit(solution)/shard_map/all_gather | solution.py:8
  161.3 1.3 copy-start.1
  212.3 4.0 copy-start
  215.0 2.9 copy-start.2
  224.1 121.7 %all-gather.19.cloned.1.call-start = ((), (), s32[]{:S(2)}) async-start(), calls=%async_computation.2 | async-start | bytes 10616832 | tf_op jit(solution)/shard_map/all_gather | solution.py:8
  290.1 120.5 %all-gather.21.cloned.1.call-start = ((), (), s32[]{:S(2)}) async-start(), calls=%async_computation.3 | async-start | bytes 10616832 | tf_op jit(solution)/shard_map/all_gather | solution.py:8
  347.0 128.8 %all-gather.23.cloned.1.call-start = ((), (), s32[]{:S(2)}) async-start(), calls=%async_computation.4 | async-start | bytes 10616832 | tf_op jit(solution)/shard_map/all_gather | solution.py:8
  412.4 129.6 %all-gather.25.cloned.1.call-start = ((), (), s32[]{:S(2)}) async-start(), calls=%async_computation.5 | async-start | bytes 10616832 | tf_op jit(solution)/shard_map/all_gather | solution.py:8
  477.0 131.0 %all-gather.27.cloned.1.call-start = ((), (), s32[]{:S(2)}) async-start(), calls=%async_computation.6 | async-start | bytes 10616832 | tf_op jit(solution)/shard_map/all_gather | solution.py:8
  543.3 129.9 %all-gather.29.cloned.1.call-start = ((), (), s32[]{:S(2)}) async-start(), calls=%async_computation.7 | async-start | bytes 10616832 | tf_op jit(solution)/shard_map/all_gather | solution.py:8
  608.0 1.2 copy-start.4
  608.0 1.3 copy-start.3
  682.6 43.8 %all-to-all-start = ((f32[32,2,8,576]{3,2,1,0:T(8,128)}), f32[32,2,8,576]{3,2,1,0:T(8,128)S(1)}, u32[]{:S(2)}, u32[]{:S(2)}) async-start(f32[32,2,8,576]{3,2,1,0:T(8,128)} %select_bitcast_fusion.1), calls=%async_computation | async-start | bytes 2621440 | tf_op jit(solution)/shard_map/all_to_all | solution.py:55
Sparse Core Ops, SparseCore 0:
  9.9 127.6 all-gather.30
  224.2 56.7 all-gather.16
  290.3 55.4 all-gather.18
  347.4 63.2 all-gather.20
  412.5 63.2 all-gather.22
  477.5 64.4 all-gather.24
  543.8 64.1 all-gather.26
  609.9 63.3 all-gather.28
where the time goes:
time: 749 us; the launch traced here: 740 us
  waiting for transfers between devices  595 us (79%)
  other arithmetic  61.4 us (8%)
  local copies, waits for them, and re-layouts  38.8 us (5%)
  matrix products  19.3 us (3%)
  between operations  14.3 us (2%)
  starting transfers between devices  10.1 us (1%)
    all_gather x7, waiting for transfers between devices, from_root(): lax.all_gather(value, axis)  433 us
    all_gather x1, waiting for transfers between devices, per_device(): factor_row = lax.all_gather(factor, 'cols', axis=0, tiled=True)  128 us
    another operation x7, other arithmetic, per_device(): jax.scipy.linalg.solve_triangular(diag_block, identity, lower=True)  52.8 us
    all_to_all x1, waiting for transfers between devices, per_device(): lax.all_to_all(grid, 'cols', split_axis=0, concat_axis=2, tiled=True)  34 us
    another operation x19, local copies, waits for them, and re-layouts  18.8 us
  transfers between devices with their start and end apart: 9, of which 9 were waited for; matrix products, arithmetic and copies ran while one was open for 0% of the time, Pallas kernels for 0%

commit v1 on v0

--- a/solution.py
+++ b/solution.py
@@ -15,7 +15,9 @@
 def per_device(factor, right_side, occ_order, cabs_order):
     chain_size = lax.axis_size("chain")
     position = lax.axis_index("chain")
-    factor_row = lax.all_gather(factor, "cols", axis=0, tiled=True)
+    factor_row = jnp.concatenate(
+        lax.all_to_all(jnp.stack([factor] * lax.axis_size("cols")), "cols", 0, 0), axis=0
+    )
     aux_rows = factor_row.shape[0]
     diag_block = lax.dynamic_slice_in_dim(factor_row, position * aux_rows, aux_rows, 1)
     identity = jnp.eye(aux_rows, dtype=jnp.float32)

time: 749 us -> 971 us (1.30)
  waiting for transfers between devices: 595 us -> 801 us
  starting transfers between devices: 10.1 us -> 20.8 us
    all_to_all x0 -> x1, waiting for transfers between devices: none -> 315 us  [per_device(): lax.all_to_all(jnp.stack([factor] * lax.axis_size('cols')), 'cols', 0, 0)]
    all_gather x1 -> x0, waiting for transfers between devices: 128 us -> none  [per_device(): factor_row = lax.all_gather(factor, 'cols', axis=0, tiled=True)]
    all_gather x7, waiting for transfers between devices: 433 us -> 452 us  [from_root(): lax.all_gather(value, axis)]
    reshape x0 -> x1, local copies, waits for them, and re-layouts: none -> 11.4 us  [per_device(): jnp.concatenate(lax.all_to_all(jnp.stack([factor] * lax.axis_size('cols')...]
    unnamed x12 -> x13, local copies, waits for them, and re-layouts: 12.7 us -> 1.39 us
    all_to_all x0 -> x1, starting transfers between devices: none -> 10.7 us  [per_device(): lax.all_to_all(jnp.stack([factor] * lax.axis_size('cols')), 'cols', 0, 0)]
    another operation x19 -> x20, local copies, waits for them, and re-layouts: 18.8 us -> 25.8 us
where the time goes in v1:
time: 971 us; the launch traced here: 964 us
  waiting for transfers between devices  801 us (82%)
  other arithmetic  61.5 us (6%)
  local copies, waits for them, and re-layouts  45.9 us (5%)
  starting transfers between devices  20.8 us (2%)
  matrix products  19.3 us (2%)
  between operations  14.3 us (1%)
    all_gather x7, waiting for transfers between devices, from_root(): lax.all_gather(value, axis)  452 us
    all_to_all x1, waiting for transfers between devices, per_device(): lax.all_to_all(jnp.stack([factor] * lax.axis_size('cols')), 'cols', 0, 0)  315 us
    another operation x7, other arithmetic, per_device(): jax.scipy.linalg.solve_triangular(diag_block, identity, lower=True)  52.8 us
    all_to_all x1, waiting for transfers between devices, per_device(): lax.all_to_all(grid, 'cols', split_axis=0, concat_axis=2, tiled=True)  34 us
  transfers between devices with their start and end apart: 9, of which 9 were waited for; matrix products, arithmetic and copies ran while one was open for 0% of the time, Pallas kernels for 0%

profile of v1, /device:TPU:33, one launch (start us, length us, event | category | flops | bytes accessed | tf_op | source)
XLA Modules:
  0.0 963.5 jit_solution(696763191808955021)
XLA Ops:
  7.9 6.8 stack.2
  14.7 10.7 %all-to-all-start = ((f32[32,18,4608]{2,1,0:T(8,128)}), f32[32,18,4608]{2,1,0:T(8,128)}, u32[]{:S(2)}, u32[]{:S(2)}) async-start(f32[32,18,4608]{2,1,0:T(8,128)} %stack.2), calls=%async_computation | async-start | bytes 28311552 | tf_op jit(solution)/shard_map/all_to_all | solution.py:19
  26.8 314.5 %all-to-all-done = f32[32,18,4608]{2,1,0:T(8,128)} async-done(((f32[32,18,4608]{2,1,0:T(8,128)}), f32[32,18,4608]{2,1,0:T(8,128)}, u32[]{:S(2)}, u32[]{:S(2)}) %all-to-all-start) | async-done | bytes 10616864 | tf_op jit(solution)/shard_map/all_to_all | solution.py:19
  341.4 11.4 %reshape.44 = f32[576,4608]{1,0:T(8,128)} reshape(f32[32,18,4608]{2,1,0:T(8,128)} %all-to-all-done) | data formatting | bytes 21233664 | tf_op jit(solution)/shard_map/reshape | solution.py:18
  354.5 10.8 %while.1 = (s32[]{:T(128)}, f32[576,576]{1,0:T(8,128)S(1)}, s32[4,2]{0,1:T(2,128)S(1)}, f32[4,128,128]{2,1,0:T(8,128)}, s32[]{:T(128)}) while((s32[]{:T(128)}, f32[576,576]{1,0:T(8,128)S(1)}, s32[4,2]{0,1:T(2,128)S(1)}, f32[4,128,128]{2,1,0:T(8,128)}, s32[]{:T(128)}) %tuple.161), condition=%wide.while_cond, body=%wide.while_body.sunk | while | flops 2 | bytes 132705 | solution.py:24
  355.2 2.0 bitcast_dynamic-update-slice_fusion.2
  357.9 2.0 bitcast_dynamic-update-slice_fusion.2
  366.5 49.8 %custom-call.4 = f32[5,128,128]{1,2,0:T(8,128)} custom-call(f32[5,128,128]{2,1,0:T(8,128)S(1)} %pad_maximum_fusion), custom_call_target="InvertDiagBlocksLowerTriangular" | custom-call | tf_op jit(solution)/shard_map/jit(_solve_triangular)/triangular_solve | solution.py:24
  428.3 76.1 %all-gather.15.cloned.1.call-done = f32[4608,512]{1,0:T(8,128)} async-done(((f32[576,512]{1,0:T(8,128)}), f32[4608,512]{1,0:T(8,128)}) %all-gather.15.cloned.1.call-update) | async-done | bytes 9437200 | tf_op jit(solution)/shard_map/all_gather | solution.py:8
  504.4 4.8 conditional.16
  504.4 4.8 fusion.2
  509.2 4.1 conditional.17
  509.2 4.1 fusion.84
  513.4 55.5 %all-gather.17.cloned.1.call-done = f32[4608,512]{1,0:T(8,128)} async-done(((f32[576,512]{1,0:T(8,128)}), f32[4608,512]{1,0:T(8,128)}) %all-gather.17.cloned.1.call-update) | async-done | bytes 9437200 | tf_op jit(solution)/shard_map/all_gather | solution.py:8
  570.6 63.7 %all-gather.19.cloned.1.call-done = f32[4608,512]{1,0:T(8,128)} async-done(((f32[576,512]{1,0:T(8,128)}), f32[4608,512]{1,0:T(8,128)}) %all-gather.19.cloned.1.call-update) | async-done | bytes 9437200 | tf_op jit(solution)/shard_map/all_gather | solution.py:8
  635.6 63.4 %all-gather.21.cloned.1.call-done = f32[4608,512]{1,0:T(8,128)} async-done(((f32[576,512]{1,0:T(8,128)}), f32[4608,512]{1,0:T(8,128)}) %all-gather.21.cloned.1.call-update) | async-done | bytes 9437200 | tf_op jit(solution)/shard_map/all_gather | solution.py:8
  700.4 64.9 %all-gather.23.cloned.1.call-done = f32[4608,512]{1,0:T(8,128)} async-done(((f32[576,512]{1,0:T(8,128)}), f32[4608,512]{1,0:T(8,128)}) %all-gather.23.cloned.1.call-update) | async-done | bytes 9437200 | tf_op jit(solution)/shard_map/all_gather | solution.py:8
  766.6 64.7 %all-gather.25.cloned.1.call-done = f32[4608,512]{1,0:T(8,128)} async-done(((f32[576,512]{1,0:T(8,128)}), f32[4608,512]{1,0:T(8,128)}) %all-gather.25.cloned.1.call-update) | async-done | bytes 9437200 | tf_op jit(solution)/shard_map/all_gather | solution.py:8
  832.8 63.8 %all-gather.27.cloned.1.call-done = f32[4608,512]{1,0:T(8,128)} async-done(((f32[576,512]{1,0:T(8,128)}), f32[4608,512]{1,0:T(8,128)}) %all-gather.27.cloned.1.call-update) | async-done | bytes 9437200 | tf_op jit(solution)/shard_map/all_gather | solution.py:8
  897.9 4.9 add_add_fusion
  905.8 9.9 %all-to-all-start.1 = ((f32[32,2,8,576]{3,2,1,0:T(8,128)}), f32[32,2,8,576]{3,2,1,0:T(8,128)S(1)}, u32[]{:S(2)}, u32[]{:S(2)}) async-start(f32[32,2,8,576]{3,2,1,0:T(8,128)} %select_bitcast_fusion.1), calls=%async_computation.1 | async-start | bytes 2621440 | tf_op jit(solution)/shard_map/all_to_all | solution.py:57
  915.7 34.0 %all-to-all-done.1 = f32[32,2,8,576]{3,2,1,0:T(8,128)S(1)} async-done(((f32[32,2,8,576]{3,2,1,0:T(8,128)}), f32[32,2,8,576]{3,2,1,0:T(8,128)S(1)}, u32[]{:S(2)}, u32[]{:S(2)}) %all-to-all-start.1) | async-done | bytes 1179680 | tf_op jit(solution)/shard_map/all_to_all | solution.py:57
  950.8 2.2 gather_fusion.1
  954.1 2.2 copy.49
  (90 shorter events, 46.3 us)
Async XLA Ops:
  6.5 1.4 copy-start.2
  14.7 326.7 %all-to-all-start = ((f32[32,18,4608]{2,1,0:T(8,128)}), f32[32,18,4608]{2,1,0:T(8,128)}, u32[]{:S(2)}, u32[]{:S(2)}) async-start(f32[32,18,4608]{2,1,0:T(8,128)} %stack.2), calls=%async_computation | async-start | bytes 28311552 | tf_op jit(solution)/shard_map/all_to_all | solution.py:19
  25.4 479.1 %all-gather.15.cloned.1.call-start = ((), (), s32[]{:S(2)}) async-start(), calls=%async_computation.2 | async-start | bytes 10616832 | tf_op jit(solution)/shard_map/all_gather | solution.py:8
  365.2 1.3 copy-start.1
  416.3 4.0 copy-start
  418.9 2.9 copy-start.3
  428.2 140.7 %all-gather.17.cloned.1.call-start = ((), (), s32[]{:S(2)}) async-start(), calls=%async_computation.3 | async-start | bytes 10616832 | tf_op jit(solution)/shard_map/all_gather | solution.py:8
  513.3 121.0 %all-gather.19.cloned.1.call-start = ((), (), s32[]{:S(2)}) async-start(), calls=%async_computation.4 | async-start | bytes 10616832 | tf_op jit(solution)/shard_map/all_gather | solution.py:8
  570.6 128.5 %all-gather.21.cloned.1.call-start = ((), (), s32[]{:S(2)}) async-start(), calls=%async_computation.5 | async-start | bytes 10616832 | tf_op jit(solution)/shard_map/all_gather | solution.py:8
  635.5 129.8 %all-gather.23.cloned.1.call-start = ((), (), s32[]{:S(2)}) async-start(), calls=%async_computation.6 | async-start | bytes 10616832 | tf_op jit(solution)/shard_map/all_gather | solution.py:8
  700.4 130.9 %all-gather.25.cloned.1.call-start = ((), (), s32[]{:S(2)}) async-start(), calls=%async_computation.7 | async-start | bytes 10616832 | tf_op jit(solution)/shard_map/all_gather | solution.py:8
  766.6 130.1 %all-gather.27.cloned.1.call-start = ((), (), s32[]{:S(2)}) async-start(), calls=%async_computation.8 | async-start | bytes 10616832 | tf_op jit(solution)/shard_map/all_gather | solution.py:8
  831.3 1.4 copy-start.5
  831.3 1.5 copy-start.4
  905.8 43.8 %all-to-all-start.1 = ((f32[32,2,8,576]{3,2,1,0:T(8,128)}), f32[32,2,8,576]{3,2,1,0:T(8,128)S(1)}, u32[]{:S(2)}, u32[]{:S(2)}) async-start(f32[32,2,8,576]{3,2,1,0:T(8,128)} %select_bitcast_fusion.1), calls=%async_computation.1 | async-start | bytes 2621440 | tf_op jit(solution)/shard_map/all_to_all | solution.py:57
Sparse Core Ops, SparseCore 0:
  428.4 76.0 all-gather.14
  513.5 55.4 all-gather.16
  570.8 63.4 all-gather.18
  636.0 63.0 all-gather.20
  700.7 64.5 all-gather.22
  767.0 64.1 all-gather.24
  833.1 63.5 all-gather.26
